TPU v7x, 32 devices: a whole 2x2x4 slice. The times are simulated.
32 devices in a mesh: seq: 8 (over y, x, core), head: 4 (over z).
Axes of the slice: x: 2, y: 2, z: 4, core: 2. Of those that a mesh axis runs over, the one named last changes fastest.
Arguments:
- query_lin: bfloat16 [512, 4096], P('seq', 'head'), may hold values from -6 to 6
- key_lin: bfloat16 [512, 4096], P('seq', 'head'), may hold values from -6 to 6
- value_lin: bfloat16 [512, 4096], P('seq', 'head'), may hold values from -6 to 6
- log_decay: float32 [32, 512], P('head', 'seq'), may hold values from -1.6 to 0
- query_soft: bfloat16 [512, 4096], P(('seq', 'head')), may hold values from -4.5 to 4.5
- key_soft: bfloat16 [512, 512], P(('seq', 'head')), may hold values from -4.5 to 4.5
- value_soft: bfloat16 [512, 512], P(('seq', 'head')), may hold values from -6 to 6
- doc_start: int32 [512], P('seq'), may hold values from 0 to 480, as said below
Outputs:
- lin_out: bfloat16 [512, 4096], P('seq', 'head')
- soft_out: bfloat16 [512, 4096], P('seq', 'head')
- soft_lse: float32 [32, 512], P('head', 'seq')
Inputs may be any that keep to these rules, and one draw needn't show every extreme that they name: doc_start[t] is the first position of the document that holds token t: 0 for the first document, never above t, the same over a document; at most 4 documents; every document but the first and the last starts at a position of 1 to 32; the last document starts at 480.
All inputs are finite; a program needn't handle non-finite values.
Results may differ from a plain program's by a relative error of at most 0.003.
Values may be sent and summed in bfloat16 or wider, within the bound.
A program may use at most 256 MiB of HBM per device.

v0:
```python
import jax
import jax.numpy as jnp
from jax import lax
from jax.sharding import PartitionSpec as P

DH = 128
HIGHEST = lax.Precision.HIGHEST
masked_score = -1e30


def prefix(array, axis, combine, identity):
    size, here = (lax.axis_size(axis), lax.axis_index(axis))
    everything = jax.tree.map(lambda part: lax.all_gather(part, axis), array)
    start = jax.tree.map(
        lambda part, zero: jnp.broadcast_to(jnp.asarray(zero, part.dtype), part.shape),
        array,
        identity,
    )

    def lap(k, before):
        reached = k < here
        new = combine(before, jax.tree.map(lambda part: part[k], everything))
        return jax.tree.map(lambda a, b: jnp.where(reached, a, b), new, before)

    return lax.fori_loop(0, size, lap, start)


def span_terms(query_heads, key_heads, value_heads, decay_rows, doc_rows, first_place):
    span_len = query_heads.shape[0]
    cumulative = jnp.cumsum(decay_rows, axis=1)
    totals = cumulative[:, -1]
    token_positions = first_place + jnp.arange(span_len, dtype=jnp.int32)
    allowed = (token_positions[None, :] <= token_positions[:, None]) & (
        doc_rows[:, None] <= token_positions[None, :]
    )
    decay_gap = jnp.where(allowed[None], cumulative[:, :, None] - cumulative[:, None, :], 0.0)
    decay_mat = jnp.where(allowed[None], jnp.exp(decay_gap), 0.0)
    scores = jnp.einsum("thd,shd->hts", query_heads, key_heads, preferred_element_type=jnp.float32)
    key_float = key_heads.astype(jnp.float32)
    value_float = value_heads.astype(jnp.float32)
    inner_part = jnp.einsum("hts,shd->thd", scores * decay_mat, value_float, precision=HIGHEST)
    keep_mask = (doc_rows == doc_rows[-1]).astype(jnp.float32)
    tail_weight = jnp.exp(totals[:, None] - cumulative) * keep_mask[None, :]
    weighted_keys = key_float * jnp.transpose(tail_weight)[:, :, None]
    fresh_state = jnp.einsum("shd,she->hde", weighted_keys, value_float, precision=HIGHEST)
    carry_on = (doc_rows[-1] < first_place).astype(jnp.float32)
    factor = jnp.exp(totals) * carry_on
    read_mask = (doc_rows < first_place).astype(jnp.float32)[:, None] * jnp.transpose(
        jnp.exp(cumulative)
    )
    return (inner_part, fresh_state, factor, read_mask)


def combine_states(earlier, later_part):
    return (earlier[0] * later_part[0], later_part[0][:, None, None] * earlier[1] + later_part[1])


def lightning_part(query_lin, key_lin, value_lin, log_decay, doc_start):
    span_len = query_lin.shape[0]
    head_count = log_decay.shape[0]
    first_place = lax.axis_index("seq") * span_len
    query_heads = query_lin.reshape(span_len, head_count, DH)
    key_heads = key_lin.reshape(span_len, head_count, DH)
    value_heads = value_lin.reshape(span_len, head_count, DH)
    inner_part, fresh_state, factor, read_mask = span_terms(
        query_heads, key_heads, value_heads, log_decay, doc_start, first_place
    )
    identity = (jnp.ones((head_count,), jnp.float32), jnp.zeros((head_count, DH, DH), jnp.float32))
    unused, carried = prefix((factor, fresh_state), "seq", combine_states, identity)
    outer_part = (
        jnp.einsum("thd,hde->the", query_heads.astype(jnp.float32), carried, precision=HIGHEST)
        * read_mask[:, :, None]
    )
    mixed_out = inner_part + outer_part
    normed = mixed_out * lax.rsqrt(jnp.mean(mixed_out * mixed_out, axis=-1, keepdims=True) + 1e-06)
    return normed.astype(jnp.bfloat16).reshape(span_len, head_count * DH)


def softmax_part(query_soft, key_soft, value_soft, doc_start):
    queries, keys_local, values_local = (
        lax.all_to_all(query_soft, "head", split_axis=1, concat_axis=0, tiled=True),
        lax.all_to_all(key_soft, "head", split_axis=1, concat_axis=0, tiled=True),
        lax.all_to_all(value_soft, "head", split_axis=1, concat_axis=0, tiled=True),
    )
    span_len = queries.shape[0]
    kv_count = keys_local.shape[1] // DH
    group_size = queries.shape[1] // keys_local.shape[1]
    first_place = lax.axis_index("seq") * span_len
    query_places = first_place + jnp.arange(span_len, dtype=jnp.int32)
    query_heads = queries.reshape(span_len, kv_count, group_size, DH)
    score_scale = DH ** (-0.5)
    start_state = (
        jnp.full((span_len, kv_count, group_size), masked_score, jnp.float32),
        jnp.zeros((span_len, kv_count, group_size), jnp.float32),
        jnp.zeros((span_len, kv_count, group_size, DH), jnp.float32),
    )
    key_piece = lax.all_gather(keys_local, "seq", axis=0, tiled=True)
    value_piece = lax.all_gather(values_local, "seq", axis=0, tiled=True)
    piece_rows = key_piece.shape[0]
    block_rows = max(
        (divisor for divisor in range(1, min(piece_rows, 1024) + 1) if piece_rows % divisor == 0)
    )
    block_count = piece_rows // block_rows
    key_parts = key_piece.reshape(block_count, block_rows, kv_count, DH)
    value_parts = value_piece.reshape(block_count, block_rows, kv_count, DH)
    begin_rows = jnp.int32(0) + block_rows * jnp.arange(block_count, dtype=jnp.int32)

    def absorb_block(running, slices):
        key_block, value_block, begin_row = slices
        running_max, norm_sum, accum_out = running
        token_positions = begin_row + jnp.arange(block_rows, dtype=jnp.int32)
        allowed = (token_positions[None, :] <= query_places[:, None]) & (
            doc_start[:, None] <= token_positions[None, :]
        )
        allowed = allowed[:, None, None, :]
        scores = (
            jnp.einsum("tkgd,skd->tkgs", query_heads, key_block, preferred_element_type=jnp.float32)
            * score_scale
        )
        new_max = jnp.maximum(
            running_max, jnp.max(jnp.where(allowed, scores, masked_score), axis=-1)
        )
        raw_weight = jnp.where(allowed, jnp.exp(scores - new_max[..., None]), 0.0)
        shrink = jnp.exp(running_max - new_max)
        norm_sum = norm_sum * shrink + jnp.sum(raw_weight, axis=-1)
        accum_out = accum_out * shrink[..., None] + jnp.einsum(
            "tkgs,skd->tkgd",
            raw_weight.astype(jnp.bfloat16),
            value_block,
            preferred_element_type=jnp.float32,
        )
        running = (new_max, norm_sum, accum_out)
        return (running, None)

    final_state, unused = lax.scan(absorb_block, start_state, (key_parts, value_parts, begin_rows))
    running_max, norm_sum, accum_out = final_state
    soft_out = (
        (accum_out / norm_sum[..., None])
        .astype(jnp.bfloat16)
        .reshape(span_len, kv_count * group_size * DH)
    )
    soft_lse = jnp.transpose(
        (running_max + jnp.log(norm_sum)).reshape(span_len, kv_count * group_size)
    )
    return (soft_out, soft_lse)


def per_device(
    query_lin, key_lin, value_lin, log_decay, query_soft, key_soft, value_soft, doc_start
):
    lin_out = lightning_part(query_lin, key_lin, value_lin, log_decay, doc_start)
    soft_out, soft_lse = softmax_part(query_soft, key_soft, value_soft, doc_start)
    return (lin_out, soft_out, soft_lse)


def solution(mesh):
    return jax.shard_map(
        per_device,
        mesh=mesh,
        in_specs=(
            P("seq", "head"),
            P("seq", "head"),
            P("seq", "head"),
            P("head", "seq"),
            P(("seq", "head"), None),
            P(("seq", "head"), None),
            P(("seq", "head"), None),
            P("seq"),
        ),
        out_specs=(P("seq", "head"), P("seq", "head"), P("head", "seq")),
        check_vma=False,
    )
```

profile of v0, /device:TPU:0, one launch (start us, length us, event | category | flops | bytes accessed | tf_op | source)
XLA Modules:
  0.0 91.8 jit_solution(14963114871208304785)
XLA Ops:
  7.2 0.0 copy-start
  7.2 0.0 all-gather.4.cloned.1.call-start
  7.2 1.2 %slice.8 = s32[1]{0:T(128)} slice(s32[64]{0:T(128)} %param.17), slice={[63:64]} | slice | bytes 8 | tf_op jit(solution)/shard_map/slice | solution.py:46
  9.1 1.3 %compare_convert_fusion = (f32[64]{0:T(128)S(1)}, f32[64]{0:T(128)S(1)}) fusion(s32[64]{0:T(128)} %param.17, s32[]{:T(128)S(6)} %mul.138, s32[]{:T(128)} %bitcast.1), kind=kLoop, calls=%fused_computation.64 | loop fusion | flops 256 | bytes 776 | tf_op jit(solution)/shard_map/convert_element_type | solution.py:48
  10.4 0.9 reduce_window_sum.11
  11.3 0.2 slice_reduce_fusion
  11.5 0.1 multiply_bitcast_fusion
  11.6 0.0 copy-done
  11.6 2.4 %fusion.11 = f32[8,128,128]{2,1,0:T(8,128)} fusion(f32[64,8]{0,1:T(8,128)S(1)} %get-tuple-element.160, bf16[64,1024]{1,0:T(8,128)(2,1)S(1)} %copy-done, bf16[64,1024]{1,0:T(8,128)(2,1)} %param.11), kind=kOutput, calls=%fused_computation.22 | convolution fusion | flops 100794368 | bytes 788480 | tf_op jit(solution)/shard_map/shd,she->hde/dot_general | solution.py:45
  14.0 0.0 all-gather.4.cloned.1.call-update
  14.0 1.3 %copy_bitcast_fusion.4 = bf16[16,4,128]{2,0,1:T(8,128)(2,1)} fusion(bf16[16,512]{1,0:T(8,128)(2,1)} %param.15), kind=kLoop, calls=%fused_computation.50 | loop fusion | bytes 32768 | tf_op jit(solution)/shard_map/all_to_all | solution.py:82
  15.3 6.3 %all-to-all-start = ((bf16[16,4,128]{2,0,1:T(8,128)(2,1)}), bf16[16,4,128]{2,0,1:T(8,128)(2,1)S(1)}, u32[]{:S(2)}, u32[]{:S(2)}) async-start(bf16[16,4,128]{2,0,1:T(8,128)(2,1)} %copy_bitcast_fusion.4), calls=%async_computation | async-start | bytes 32768 | tf_op jit(solution)/shard_map/all_to_all | solution.py:82
  21.7 1.3 %copy_bitcast_fusion.3 = bf16[16,4,128]{2,0,1:T(8,128)(2,1)} fusion(bf16[16,512]{1,0:T(8,128)(2,1)} %param.16), kind=kLoop, calls=%fused_computation.49 | loop fusion | bytes 32768 | tf_op jit(solution)/shard_map/all_to_all | solution.py:83
  23.0 0.7 compare_and_fusion
  23.7 3.5 %all-to-all-done = bf16[16,4,128]{2,0,1:T(8,128)(2,1)S(1)} async-done(((bf16[16,4,128]{2,0,1:T(8,128)(2,1)}), bf16[16,4,128]{2,0,1:T(8,128)(2,1)S(1)}, u32[]{:S(2)}, u32[]{:S(2)}) %all-to-all-start) | async-done | bytes 16416 | tf_op jit(solution)/shard_map/all_to_all | solution.py:82
  27.3 3.3 %all-to-all-start.2 = ((bf16[16,4,128]{2,0,1:T(8,128)(2,1)}), bf16[16,4,128]{2,0,1:T(8,128)(2,1)S(1)}, u32[]{:S(2)}, u32[]{:S(2)}) async-start(bf16[16,4,128]{2,0,1:T(8,128)(2,1)} %copy_bitcast_fusion.3), calls=%async_computation.2 | async-start | bytes 32768 | tf_op jit(solution)/shard_map/all_to_all | solution.py:83
  30.5 1.2 %convolution_multiply_fusion.1 = f32[8,64,64]{2,1,0:T(8,128)S(1)} fusion(f32[8,64]{1,0:T(8,128)S(1)} %reduce_window_sum.11, pred[64,64]{1,0:T(8,128)(4,1)S(1)} %compare_and_fusion, bf16[64,1024]{1,0:T(8,128)(2,1)} %param.11, bf16[64,1024]{1,0:T(8,128)(2,1)} %param.10), kind=kOutput, calls=%fused_computation.10 | convolution fusion | flops 8519680 | bytes 399360 | tf_op jit(solution)/shard_map/thd,shd->hts/dot_general | solution.py:38
  31.7 1.2 %dynamic-slice = u32[1]{0:T(128)} dynamic-slice(u32[32]{0:T(128)} %constant.72, u32[]{:T(128)S(6)} %add.102), dynamic_slice_sizes={1} | dynamic-slice | bytes 12
  33.6 0.2 dynamic-update-slice
  33.9 12.5 %all-reduce = f32[64]{0:T(128)S(1)} all-reduce(f32[64]{0:T(128)S(1)} %dynamic-update-slice), channel_id=2, replica_groups=mesh['seq'=8,'head'=4] {'seq'}, use_global_device_ids=true, to_apply=%add | all-reduce | flops 64 | bytes 512
  46.4 0.1 reshape.236
  46.5 1.6 %copy.93 = bf16[2,4,8,1024]{3,2,0,1:T(8,128)(2,1)} copy(bf16[2,4,8,1024]{3,2,1,0:T(8,128)(2,1)} %bitcast.145) | data formatting | bytes 262144 | tf_op jit(solution)/shard_map/all_to_all | solution.py:81
  48.1 0.0 all-to-all-done.2
  48.1 4.8 %all-to-all-start.1 = ((bf16[16,4,1024]{2,0,1:T(8,128)(2,1)}), bf16[16,4,1024]{2,0,1:T(8,128)(2,1)S(1)}, u32[]{:S(2)}, u32[]{:S(2)}) async-start(bf16[16,4,1024]{2,0,1:T(8,128)(2,1)} %bitcast.137), calls=%async_computation.1 | async-start | bytes 262144 | tf_op jit(solution)/shard_map/all_to_all | solution.py:81
  52.8 0.7 fusion.25
  53.6 9.1 %all_gather.19 = bf16[512,128]{1,0:T(8,128)(2,1)S(1)} all-gather(bf16[64,128]{1,0:T(8,128)(2,1)S(1)} %bitcast.148), channel_id=1, replica_groups=mesh['seq'=8,'head'=4] {'seq'}, dimensions={0}, use_global_device_ids=true | all-gather | bytes 147456 | tf_op jit(solution)/shard_map/all_gather | solution.py:97
  62.7 8.4 %all_gather.20 = bf16[512,128]{1,0:T(8,128)(2,1)S(1)} all-gather(bf16[64,128]{1,0:T(8,128)(2,1)S(1)} %bitcast.149), channel_id=1, replica_groups=mesh['seq'=8,'head'=4] {'seq'}, dimensions={0}, use_global_device_ids=true | all-gather | bytes 147456 | tf_op jit(solution)/shard_map/all_gather | solution.py:98
  71.0 0.0 all-to-all-done.1
  71.1 0.4 select_reduce_fusion
  71.4 0.4 fusion.7
  71.8 0.1 copy.42
  71.9 0.1 copy.45
  72.0 0.5 fusion.6
  72.5 0.0 copy-start.1
  72.5 0.7 copy.92
  73.1 0.6 fusion.33
  73.8 0.0 all-gather.4.cloned.1.call-done
  73.8 9.7 %while.9 = (s32[]{:T(128)}, f32[8,128,128]{2,1,0:T(8,128)S(1)}, s32[]{:T(128)}, f32[8,8]{1,0:T(8,128)S(1)}, f32[8,8,128,128]{3,2,1,0:T(8,128)}, /*index=5*/s32[]{:T(128)}, s32[]{:T(128)}) while((s32[]{:T(128)}, f32[8,128,128]{2,1,0:T(8,128)S(1)}, s32[]{:T(128)}, f32[8,8]{1,0:T(8,128)S(1)}, f32[8,8,128,128]{3,2,1,0:T(8,128)}, ...), condition=%wide.region_2.3_spmd.clone, body=%wide.region_1.2_spmd.clone.sunk | while | flops 524292 | bytes 1573065 | solution.py:25
  73.8 1.2 %fusion.49 = f32[8,128,128]{2,1,0:T(8,128)S(1)} fusion(f32[8,8,128,128]{3,2,1,0:T(8,128)} %get-tuple-element.216, s32[]{:T(128)} %get-tuple-element.205, f32[8,128,128]{2,1,0:T(8,128)S(1)} %get-tuple-element.206, f32[8]{0:T(128)S(1)} %dynamic-slice_bitcast_fusion.2, pred[]{:T(512)S(6)} %compare.3, pred[]{:T(512)S(6)} %lt.33), kind=kLoop, calls=%fused_computation.1.clone.1 | loop fusion | flops 524288 | bytes 1572902 | tf_op jit(solution)/shard_map/while/body/eval_jaxpr/jit(_where)/select_n | solution.py:23
  75.0 1.2 %fusion.49 = f32[8,128,128]{2,1,0:T(8,128)S(1)} fusion(f32[8,8,128,128]{3,2,1,0:T(8,128)} %get-tuple-element.216, s32[]{:T(128)} %get-tuple-element.205, f32[8,128,128]{2,1,0:T(8,128)S(1)} %get-tuple-element.206, f32[8]{0:T(128)S(1)} %dynamic-slice_bitcast_fusion.2, pred[]{:T(512)S(6)} %compare.3, pred[]{:T(512)S(6)} %lt.33), kind=kLoop, calls=%fused_computation.1.clone.1 | loop fusion | flops 524288 | bytes 1572902 | tf_op jit(solution)/shard_map/while/body/eval_jaxpr/jit(_where)/select_n | solution.py:23
  76.2 1.2 %fusion.49 = f32[8,128,128]{2,1,0:T(8,128)S(1)} fusion(f32[8,8,128,128]{3,2,1,0:T(8,128)} %get-tuple-element.216, s32[]{:T(128)} %get-tuple-element.205, f32[8,128,128]{2,1,0:T(8,128)S(1)} %get-tuple-element.206, f32[8]{0:T(128)S(1)} %dynamic-slice_bitcast_fusion.2, pred[]{:T(512)S(6)} %compare.3, pred[]{:T(512)S(6)} %lt.33), kind=kLoop, calls=%fused_computation.1.clone.1 | loop fusion | flops 524288 | bytes 1572902 | tf_op jit(solution)/shard_map/while/body/eval_jaxpr/jit(_where)/select_n | solution.py:23
  77.4 1.2 %fusion.49 = f32[8,128,128]{2,1,0:T(8,128)S(1)} fusion(f32[8,8,128,128]{3,2,1,0:T(8,128)} %get-tuple-element.216, s32[]{:T(128)} %get-tuple-element.205, f32[8,128,128]{2,1,0:T(8,128)S(1)} %get-tuple-element.206, f32[8]{0:T(128)S(1)} %dynamic-slice_bitcast_fusion.2, pred[]{:T(512)S(6)} %compare.3, pred[]{:T(512)S(6)} %lt.33), kind=kLoop, calls=%fused_computation.1.clone.1 | loop fusion | flops 524288 | bytes 1572902 | tf_op jit(solution)/shard_map/while/body/eval_jaxpr/jit(_where)/select_n | solution.py:23
  78.6 1.2 %fusion.49 = f32[8,128,128]{2,1,0:T(8,128)S(1)} fusion(f32[8,8,128,128]{3,2,1,0:T(8,128)} %get-tuple-element.216, s32[]{:T(128)} %get-tuple-element.205, f32[8,128,128]{2,1,0:T(8,128)S(1)} %get-tuple-element.206, f32[8]{0:T(128)S(1)} %dynamic-slice_bitcast_fusion.2, pred[]{:T(512)S(6)} %compare.3, pred[]{:T(512)S(6)} %lt.33), kind=kLoop, calls=%fused_computation.1.clone.1 | loop fusion | flops 524288 | bytes 1572902 | tf_op jit(solution)/shard_map/while/body/eval_jaxpr/jit(_where)/select_n | solution.py:23
  79.8 1.2 %fusion.49 = f32[8,128,128]{2,1,0:T(8,128)S(1)} fusion(f32[8,8,128,128]{3,2,1,0:T(8,128)} %get-tuple-element.216, s32[]{:T(128)} %get-tuple-element.205, f32[8,128,128]{2,1,0:T(8,128)S(1)} %get-tuple-element.206, f32[8]{0:T(128)S(1)} %dynamic-slice_bitcast_fusion.2, pred[]{:T(512)S(6)} %compare.3, pred[]{:T(512)S(6)} %lt.33), kind=kLoop, calls=%fused_computation.1.clone.1 | loop fusion | flops 524288 | bytes 1572902 | tf_op jit(solution)/shard_map/while/body/eval_jaxpr/jit(_where)/select_n | solution.py:23
  81.0 1.2 %fusion.49 = f32[8,128,128]{2,1,0:T(8,128)S(1)} fusion(f32[8,8,128,128]{3,2,1,0:T(8,128)} %get-tuple-element.216, s32[]{:T(128)} %get-tuple-element.205, f32[8,128,128]{2,1,0:T(8,128)S(1)} %get-tuple-element.206, f32[8]{0:T(128)S(1)} %dynamic-slice_bitcast_fusion.2, pred[]{:T(512)S(6)} %compare.3, pred[]{:T(512)S(6)} %lt.33), kind=kLoop, calls=%fused_computation.1.clone.1 | loop fusion | flops 524288 | bytes 1572902 | tf_op jit(solution)/shard_map/while/body/eval_jaxpr/jit(_where)/select_n | solution.py:23
  82.2 1.2 %fusion.49 = f32[8,128,128]{2,1,0:T(8,128)S(1)} fusion(f32[8,8,128,128]{3,2,1,0:T(8,128)} %get-tuple-element.216, s32[]{:T(128)} %get-tuple-element.205, f32[8,128,128]{2,1,0:T(8,128)S(1)} %get-tuple-element.206, f32[8]{0:T(128)S(1)} %dynamic-slice_bitcast_fusion.2, pred[]{:T(512)S(6)} %compare.3, pred[]{:T(512)S(6)} %lt.33), kind=kLoop, calls=%fused_computation.1.clone.1 | loop fusion | flops 524288 | bytes 1572902 | tf_op jit(solution)/shard_map/while/body/eval_jaxpr/jit(_where)/select_n | solution.py:23
  83.4 0.0 copy-done.1
  83.4 0.4 fusion.2
  83.8 0.4 multiply_reduce_fusion
  84.2 0.8 copy_bitcast_fusion.1
  (15 shorter events, 0.1 us)
Async XLA Ops:
  7.2 4.4 %copy-start = (bf16[64,1024]{1,0:T(8,128)(2,1)S(1)}, bf16[64,1024]{1,0:T(8,128)(2,1)}, u32[]{:S(2)}) copy-start(bf16[64,1024]{1,0:T(8,128)(2,1)} %param.12) | copy-start | bytes 393220
  7.2 66.6 %all-gather.4.cloned.1.call-start = ((), (), s32[]{:S(2)}) async-start(), calls=%async_computation.3 | async-start | bytes 4718592 | tf_op jit(solution)/shard_map/all_gather | solution.py:13
  15.3 11.9 %all-to-all-start = ((bf16[16,4,128]{2,0,1:T(8,128)(2,1)}), bf16[16,4,128]{2,0,1:T(8,128)(2,1)S(1)}, u32[]{:S(2)}, u32[]{:S(2)}) async-start(bf16[16,4,128]{2,0,1:T(8,128)(2,1)} %copy_bitcast_fusion.4), calls=%async_computation | async-start | bytes 32768 | tf_op jit(solution)/shard_map/all_to_all | solution.py:82
  27.3 20.8 %all-to-all-start.2 = ((bf16[16,4,128]{2,0,1:T(8,128)(2,1)}), bf16[16,4,128]{2,0,1:T(8,128)(2,1)S(1)}, u32[]{:S(2)}, u32[]{:S(2)}) async-start(bf16[16,4,128]{2,0,1:T(8,128)(2,1)} %copy_bitcast_fusion.3), calls=%async_computation.2 | async-start | bytes 32768 | tf_op jit(solution)/shard_map/all_to_all | solution.py:83
  48.1 23.0 %all-to-all-start.1 = ((bf16[16,4,1024]{2,0,1:T(8,128)(2,1)}), bf16[16,4,1024]{2,0,1:T(8,128)(2,1)S(1)}, u32[]{:S(2)}, u32[]{:S(2)}) async-start(bf16[16,4,1024]{2,0,1:T(8,128)(2,1)} %bitcast.137), calls=%async_computation.1 | async-start | bytes 262144 | tf_op jit(solution)/shard_map/all_to_all | solution.py:81
  72.5 11.0 %copy-start.1 = (bf16[64,1024]{1,0:T(8,128)(2,1)S(1)}, bf16[64,1024]{1,0:T(8,128)(2,1)}, u32[]{:S(2)}) copy-start(bf16[64,1024]{1,0:T(8,128)(2,1)} %param.10) | copy-start | bytes 393220
Sparse Core Ops, SparseCore 0:
  14.1 39.5 all-gather.3
where the time goes:
time: 92.9 us; the launch traced here: 91.8 us
  blocking collectives  30 us (32%)
  between operations  15.5 us (17%)
  other arithmetic  15.1 us (16%)
  starting transfers between devices  14.4 us (16%)
  local copies, waits for them, and re-layouts  7.97 us (9%)
  matrix products  5.12 us (6%)
  waiting for transfers between devices  3.56 us (4%)
    unnamed x1, blocking collectives  12.5 us
    select_n x8, other arithmetic, lap(): return jax.tree.map(lambda a, b: jnp.where(reached, a, b), new, before)  9.38 us
    all_gather x1, blocking collectives, softmax_part(): key_piece = lax.all_gather(keys_local, 'seq', axis=0, tiled=True)  9.07 us
    all_gather x1, blocking collectives, softmax_part(): value_piece = lax.all_gather(values_local, 'seq', axis=0, tiled=True)  8.36 us
    all_to_all x1, starting transfers between devices, softmax_part(): lax.all_to_all(key_soft, 'head', split_axis=1, concat_axis=0, tiled=True)  6.32 us
    all_to_all x1, starting transfers between devices, softmax_part(): lax.all_to_all(query_soft, 'head', split_axis=1, concat_axis=0, tiled=True)  4.78 us
    all_to_all x1, waiting for transfers between devices, softmax_part(): lax.all_to_all(key_soft, 'head', split_axis=1, concat_axis=0, tiled=True)  3.54 us
    all_to_all x1, starting transfers between devices, softmax_part(): lax.all_to_all(value_soft, 'head', split_axis=1, concat_axis=0, tiled=True)  3.25 us
  transfers between devices with their start and end apart: 4, of which 1 were waited for; matrix products, arithmetic and copies ran while one was open for 12% of the time, Pallas kernels for 0%

commit v1 on v0

--- a/solution.py
+++ b/solution.py
@@ -94,7 +94,12 @@
         jnp.zeros((span_len, kv_count, group_size), jnp.float32),
         jnp.zeros((span_len, kv_count, group_size, DH), jnp.float32),
     )
-    key_piece = lax.all_gather(keys_local, "seq", axis=0, tiled=True)
+    ring = [keys_local]
+    for hop in range(7):
+        ring.append(lax.ppermute(ring[-1], "seq", [(dev, (dev + 1) % 8) for dev in range(8)]))
+    key_piece = jnp.roll(
+        jnp.concatenate(ring[::-1], axis=0), (lax.axis_index("seq") + 1) * ring[0].shape[0], axis=0
+    )
     value_piece = lax.all_gather(values_local, "seq", axis=0, tiled=True)
     piece_rows = key_piece.shape[0]
     block_rows = max(

time: 92.9 us -> 104 us (1.12)
  waiting for transfers between devices: 3.56 us -> 14.6 us
  blocking collectives: 30 us -> 35.4 us
  starting transfers between devices: 14.4 us -> 9.12 us
    ppermute x0 -> x7, waiting for transfers between devices: none -> 14.5 us  [softmax_part(): lax.ppermute(ring[-1], 'seq', [(dev, (dev + 1) % 8) for dev in range(8)])]
    all_to_all x0 -> x1, blocking collectives: none -> 11.7 us  [softmax_part(): lax.all_to_all(key_soft, 'head', split_axis=1, concat_axis=0, tiled=True)]
    all_gather x1 -> x0, blocking collectives: 9.07 us -> none  [softmax_part(): key_piece = lax.all_gather(keys_local, 'seq', axis=0, tiled=True)]
    all_to_all x1 -> x0, starting transfers between devices: 6.32 us -> none  [softmax_part(): lax.all_to_all(key_soft, 'head', split_axis=1, concat_axis=0, tiled=True)]
    all_to_all x1 -> x0, waiting for transfers between devices: 3.54 us -> none  [softmax_part(): lax.all_to_all(key_soft, 'head', split_axis=1, concat_axis=0, tiled=True)]
    unnamed x1, blocking collectives: 12.5 us -> 14.4 us
    unnamed x9 -> x24, local copies, waits for them, and re-layouts: 2.2 us -> 2.33 us
  transfers between devices with their start and end apart: 4 -> 10, of which waited for: 1 -> 4; matrix products, arithmetic and copies ran while one was open for 12% -> 10% of each run, Pallas kernels for 0% -> 0%
where the time goes in v1:
time: 104 us; the launch traced here: 103 us
  blocking collectives  35.4 us (34%)
  between operations  15.6 us (15%)
  other arithmetic  15.1 us (15%)
  waiting for transfers between devices  14.6 us (14%)
  starting transfers between devices  9.12 us (9%)
  local copies, waits for them, and re-layouts  7.51 us (7%)
  matrix products  5.14 us (5%)
    ppermute x7, waiting for transfers between devices, softmax_part(): lax.ppermute(ring[-1], 'seq', [(dev, (dev + 1) % 8) for dev in range(8)])  14.5 us
    unnamed x1, blocking collectives  14.4 us
    all_to_all x1, blocking collectives, softmax_part(): lax.all_to_all(key_soft, 'head', split_axis=1, concat_axis=0, tiled=True)  11.7 us
    select_n x8, other arithmetic, lap(): return jax.tree.map(lambda a, b: jnp.where(reached, a, b), new, before)  9.38 us
    all_gather x1, blocking collectives, softmax_part(): value_piece = lax.all_gather(values_local, 'seq', axis=0, tiled=True)  9.32 us
    all_to_all x1, starting transfers between devices, softmax_part(): lax.all_to_all(query_soft, 'head', split_axis=1, concat_axis=0, tiled=True)  5.06 us
    all_to_all x1, starting transfers between devices, softmax_part(): lax.all_to_all(value_soft, 'head', split_axis=1, concat_axis=0, tiled=True)  3.25 us
    dot_general x1, matrix products, span_terms(): jnp.einsum('shd,she->hde', weighted_keys, value_float, precision=HIGHEST)  2.4 us
  transfers between devices with their start and end apart: 10, of which 4 were waited for; matrix products, arithmetic and copies ran while one was open for 10% of the time, Pallas kernels for 0%

profile of v1, /device:TPU:0, one launch (start us, length us, event | category | flops | bytes accessed | tf_op | source)
XLA Modules:
  0.0 102.7 jit_solution(15270654322910318573)
XLA Ops:
  7.2 0.0 copy-start
  7.2 0.0 all-gather.4.cloned.1.call-start
  7.2 1.2 %slice.8 = s32[1]{0:T(128)} slice(s32[64]{0:T(128)} %param.17), slice={[63:64]} | slice | bytes 8 | tf_op jit(solution)/shard_map/slice | solution.py:46
  9.1 1.3 %compare_convert_fusion = (f32[64]{0:T(128)S(1)}, f32[64]{0:T(128)S(1)}) fusion(s32[64]{0:T(128)} %param.17, s32[]{:T(128)S(6)} %mul.141, s32[]{:T(128)} %bitcast.1), kind=kLoop, calls=%fused_computation.81 | loop fusion | flops 256 | bytes 776 | tf_op jit(solution)/shard_map/convert_element_type | solution.py:48
  10.4 0.9 reduce_window_sum.11
  11.3 0.2 slice_reduce_fusion
  11.5 0.1 multiply_bitcast_fusion
  11.6 0.0 copy-done
  11.6 2.4 %fusion.11 = f32[8,128,128]{2,1,0:T(8,128)} fusion(f32[64,8]{0,1:T(8,128)S(1)} %get-tuple-element.160, bf16[64,1024]{1,0:T(8,128)(2,1)S(1)} %copy-done, bf16[64,1024]{1,0:T(8,128)(2,1)} %param.11), kind=kOutput, calls=%fused_computation.22 | convolution fusion | flops 100794368 | bytes 788480 | tf_op jit(solution)/shard_map/shd,she->hde/dot_general | solution.py:45
  14.0 0.0 all-gather.4.cloned.1.call-update
  14.0 0.7 copy_bitcast_fusion.4
  14.7 11.7 %all_to_all.54 = bf16[16,4,128]{2,0,1:T(8,128)(2,1)S(1)} all-to-all(bf16[16,4,128]{2,0,1:T(8,128)(2,1)S(1)} %copy_bitcast_fusion.4), channel_id=1, replica_groups=mesh['seq'=8,'head'=4] {'head'}, dimensions={1} | all-to-all | bytes 32768 | tf_op jit(solution)/shard_map/all_to_all | solution.py:82
  26.5 0.0 collective-permute-start
  26.5 4.4 %collective-permute-done = bf16[64,128]{1,0:T(8,128)(2,1)S(1)} collective-permute-done((bf16[64,128]{1,0:T(8,128)(2,1)S(1)}, bf16[64,128]{1,0:T(8,128)(2,1)S(1)}, u32[]{:S(2)}, u32[]{:S(2)}) %collective-permute-start) | collective-permute-done | bytes 16416 | tf_op jit(solution)/shard_map/ppermute | solution.py:99
  30.8 0.0 collective-permute-start.1
  30.9 1.3 %copy_bitcast_fusion.3 = bf16[16,4,128]{2,0,1:T(8,128)(2,1)} fusion(bf16[16,512]{1,0:T(8,128)(2,1)} %param.16), kind=kLoop, calls=%fused_computation.66 | loop fusion | bytes 32768 | tf_op jit(solution)/shard_map/all_to_all | solution.py:83
  32.2 3.3 %all-to-all-start.2 = ((bf16[16,4,128]{2,0,1:T(8,128)(2,1)}), bf16[16,4,128]{2,0,1:T(8,128)(2,1)S(1)}, u32[]{:S(2)}, u32[]{:S(2)}) async-start(bf16[16,4,128]{2,0,1:T(8,128)(2,1)} %copy_bitcast_fusion.3), calls=%async_computation.2 | async-start | bytes 32768 | tf_op jit(solution)/shard_map/all_to_all | solution.py:83
  35.4 0.0 collective-permute-done.1
  35.4 0.8 collective-permute-start.2
  36.2 3.4 %collective-permute-done.2 = bf16[64,128]{1,0:T(8,128)(2,1)S(1)} collective-permute-done((bf16[64,128]{1,0:T(8,128)(2,1)S(1)}, bf16[64,128]{1,0:T(8,128)(2,1)S(1)}, u32[]{:S(2)}, u32[]{:S(2)}) %collective-permute-start.2) | collective-permute-done | bytes 16416 | tf_op jit(solution)/shard_map/ppermute | solution.py:99
  39.6 0.0 collective-permute-start.3
  39.6 0.7 compare_and_fusion
  40.3 3.6 %collective-permute-done.3 = bf16[64,128]{1,0:T(8,128)(2,1)S(1)} collective-permute-done((bf16[64,128]{1,0:T(8,128)(2,1)S(1)}, bf16[64,128]{1,0:T(8,128)(2,1)S(1)}, u32[]{:S(2)}, u32[]{:S(2)}) %collective-permute-start.3) | collective-permute-done | bytes 16416 | tf_op jit(solution)/shard_map/ppermute | solution.py:99
  43.9 0.0 collective-permute-start.4
  43.9 1.2 %convolution_multiply_fusion.1 = f32[8,64,64]{2,1,0:T(8,128)S(1)} fusion(f32[8,64]{1,0:T(8,128)S(1)} %reduce_window_sum.11, pred[64,64]{1,0:T(8,128)(4,1)S(1)} %compare_and_fusion, bf16[64,1024]{1,0:T(8,128)(2,1)} %param.11, bf16[64,1024]{1,0:T(8,128)(2,1)} %param.10), kind=kOutput, calls=%fused_computation.10 | convolution fusion | flops 8519680 | bytes 399360 | tf_op jit(solution)/shard_map/thd,shd->hts/dot_general | solution.py:38
  45.1 3.2 %collective-permute-done.4 = bf16[64,128]{1,0:T(8,128)(2,1)S(1)} collective-permute-done((bf16[64,128]{1,0:T(8,128)(2,1)S(1)}, bf16[64,128]{1,0:T(8,128)(2,1)S(1)}, u32[]{:S(2)}, u32[]{:S(2)}) %collective-permute-start.4) | collective-permute-done | bytes 16416 | tf_op jit(solution)/shard_map/ppermute | solution.py:99
  48.3 0.0 collective-permute-start.5
  48.3 0.7 fusion.26
  49.1 1.2 %dynamic-slice = u32[1]{0:T(128)} dynamic-slice(u32[32]{0:T(128)} %constant.95, u32[]{:T(128)S(6)} %add.118), dynamic_slice_sizes={1} | dynamic-slice | bytes 12
  51.0 0.2 dynamic-update-slice
  51.2 14.4 %all-reduce = f32[64]{0:T(128)S(1)} all-reduce(f32[64]{0:T(128)S(1)} %dynamic-update-slice), channel_id=2, replica_groups=mesh['seq'=8,'head'=4] {'seq'}, use_global_device_ids=true, to_apply=%add | all-reduce | flops 64 | bytes 512
  65.6 0.1 reshape.236
  65.7 1.6 %copy.93 = bf16[2,4,8,1024]{3,2,0,1:T(8,128)(2,1)} copy(bf16[2,4,8,1024]{3,2,1,0:T(8,128)(2,1)} %bitcast.148) | data formatting | bytes 262144 | tf_op jit(solution)/shard_map/all_to_all | solution.py:81
  67.3 0.0 collective-permute-done.5
  67.3 0.0 collective-permute-start.6
  67.3 0.0 all-to-all-done.2
  67.3 5.1 %all-to-all-start.1 = ((bf16[16,4,1024]{2,0,1:T(8,128)(2,1)}), bf16[16,4,1024]{2,0,1:T(8,128)(2,1)S(1)}, u32[]{:S(2)}, u32[]{:S(2)}) async-start(bf16[16,4,1024]{2,0,1:T(8,128)(2,1)} %bitcast.137), calls=%async_computation.1 | async-start | bytes 262144 | tf_op jit(solution)/shard_map/all_to_all | solution.py:81
  72.4 9.3 %all_gather.16 = bf16[512,128]{1,0:T(8,128)(2,1)S(1)} all-gather(bf16[64,128]{1,0:T(8,128)(2,1)S(1)} %bitcast.151), channel_id=1, replica_groups=mesh['seq'=8,'head'=4] {'seq'}, dimensions={0}, use_global_device_ids=true | all-gather | bytes 147456 | tf_op jit(solution)/shard_map/all_gather | solution.py:103
  81.7 0.0 collective-permute-done.6
  81.9 0.0 all-to-all-done.1
  81.9 0.4 select_reduce_fusion
  82.3 0.4 fusion.7
  82.7 0.1 copy.45
  82.8 0.1 copy.42
  82.9 0.4 fusion.6
  83.3 0.0 copy-start.1
  83.3 0.7 copy.92
  84.0 0.6 fusion.34
  84.6 0.0 all-gather.4.cloned.1.call-done
  84.6 9.7 %while.9 = (s32[]{:T(128)}, f32[8,128,128]{2,1,0:T(8,128)S(1)}, s32[]{:T(128)}, f32[8,8]{1,0:T(8,128)S(1)}, f32[8,8,128,128]{3,2,1,0:T(8,128)}, /*index=5*/s32[]{:T(128)}, s32[]{:T(128)}) while((s32[]{:T(128)}, f32[8,128,128]{2,1,0:T(8,128)S(1)}, s32[]{:T(128)}, f32[8,8]{1,0:T(8,128)S(1)}, f32[8,8,128,128]{3,2,1,0:T(8,128)}, ...), condition=%wide.region_2.3_spmd.clone, body=%wide.region_1.2_spmd.clone.sunk | while | flops 524292 | bytes 1573073 | solution.py:25
  84.6 1.2 %fusion.51 = f32[8,128,128]{2,1,0:T(8,128)S(1)} fusion(f32[8,8,128,128]{3,2,1,0:T(8,128)} %get-tuple-element.216, s32[]{:T(128)S(6)} %copy.97, f32[8,128,128]{2,1,0:T(8,128)S(1)} %get-tuple-element.206, f32[8]{0:T(128)S(1)} %dynamic-slice_bitcast_fusion.2, pred[]{:T(512)S(6)} %compare.4, pred[]{:T(512)S(6)} %lt.47), kind=kLoop, calls=%fused_computation.1.clone.1 | loop fusion | flops 524288 | bytes 1572902 | tf_op jit(solution)/shard_map/while/body/eval_jaxpr/jit(_where)/select_n | solution.py:23
  85.8 1.2 %fusion.51 = f32[8,128,128]{2,1,0:T(8,128)S(1)} fusion(f32[8,8,128,128]{3,2,1,0:T(8,128)} %get-tuple-element.216, s32[]{:T(128)S(6)} %copy.97, f32[8,128,128]{2,1,0:T(8,128)S(1)} %get-tuple-element.206, f32[8]{0:T(128)S(1)} %dynamic-slice_bitcast_fusion.2, pred[]{:T(512)S(6)} %compare.4, pred[]{:T(512)S(6)} %lt.47), kind=kLoop, calls=%fused_computation.1.clone.1 | loop fusion | flops 524288 | bytes 1572902 | tf_op jit(solution)/shard_map/while/body/eval_jaxpr/jit(_where)/select_n | solution.py:23
  87.1 1.2 %fusion.51 = f32[8,128,128]{2,1,0:T(8,128)S(1)} fusion(f32[8,8,128,128]{3,2,1,0:T(8,128)} %get-tuple-element.216, s32[]{:T(128)S(6)} %copy.97, f32[8,128,128]{2,1,0:T(8,128)S(1)} %get-tuple-element.206, f32[8]{0:T(128)S(1)} %dynamic-slice_bitcast_fusion.2, pred[]{:T(512)S(6)} %compare.4, pred[]{:T(512)S(6)} %lt.47), kind=kLoop, calls=%fused_computation.1.clone.1 | loop fusion | flops 524288 | bytes 1572902 | tf_op jit(solution)/shard_map/while/body/eval_jaxpr/jit(_where)/select_n | solution.py:23
  88.3 1.2 %fusion.51 = f32[8,128,128]{2,1,0:T(8,128)S(1)} fusion(f32[8,8,128,128]{3,2,1,0:T(8,128)} %get-tuple-element.216, s32[]{:T(128)S(6)} %copy.97, f32[8,128,128]{2,1,0:T(8,128)S(1)} %get-tuple-element.206, f32[8]{0:T(128)S(1)} %dynamic-slice_bitcast_fusion.2, pred[]{:T(512)S(6)} %compare.4, pred[]{:T(512)S(6)} %lt.47), kind=kLoop, calls=%fused_computation.1.clone.1 | loop fusion | flops 524288 | bytes 1572902 | tf_op jit(solution)/shard_map/while/body/eval_jaxpr/jit(_where)/select_n | solution.py:23
  89.5 1.2 %fusion.51 = f32[8,128,128]{2,1,0:T(8,128)S(1)} fusion(f32[8,8,128,128]{3,2,1,0:T(8,128)} %get-tuple-element.216, s32[]{:T(128)S(6)} %copy.97, f32[8,128,128]{2,1,0:T(8,128)S(1)} %get-tuple-element.206, f32[8]{0:T(128)S(1)} %dynamic-slice_bitcast_fusion.2, pred[]{:T(512)S(6)} %compare.4, pred[]{:T(512)S(6)} %lt.47), kind=kLoop, calls=%fused_computation.1.clone.1 | loop fusion | flops 524288 | bytes 1572902 | tf_op jit(solution)/shard_map/while/body/eval_jaxpr/jit(_where)/select_n | solution.py:23
  90.7 1.2 %fusion.51 = f32[8,128,128]{2,1,0:T(8,128)S(1)} fusion(f32[8,8,128,128]{3,2,1,0:T(8,128)} %get-tuple-element.216, s32[]{:T(128)S(6)} %copy.97, f32[8,128,128]{2,1,0:T(8,128)S(1)} %get-tuple-element.206, f32[8]{0:T(128)S(1)} %dynamic-slice_bitcast_fusion.2, pred[]{:T(512)S(6)} %compare.4, pred[]{:T(512)S(6)} %lt.47), kind=kLoop, calls=%fused_computation.1.clone.1 | loop fusion | flops 524288 | bytes 1572902 | tf_op jit(solution)/shard_map/while/body/eval_jaxpr/jit(_where)/select_n | solution.py:23
  91.9 1.2 %fusion.51 = f32[8,128,128]{2,1,0:T(8,128)S(1)} fusion(f32[8,8,128,128]{3,2,1,0:T(8,128)} %get-tuple-element.216, s32[]{:T(128)S(6)} %copy.97, f32[8,128,128]{2,1,0:T(8,128)S(1)} %get-tuple-element.206, f32[8]{0:T(128)S(1)} %dynamic-slice_bitcast_fusion.2, pred[]{:T(512)S(6)} %compare.4, pred[]{:T(512)S(6)} %lt.47), kind=kLoop, calls=%fused_computation.1.clone.1 | loop fusion | flops 524288 | bytes 1572902 | tf_op jit(solution)/shard_map/while/body/eval_jaxpr/jit(_where)/select_n | solution.py:23
  93.1 1.2 %fusion.51 = f32[8,128,128]{2,1,0:T(8,128)S(1)} fusion(f32[8,8,128,128]{3,2,1,0:T(8,128)} %get-tuple-element.216, s32[]{:T(128)S(6)} %copy.97, f32[8,128,128]{2,1,0:T(8,128)S(1)} %get-tuple-element.206, f32[8]{0:T(128)S(1)} %dynamic-slice_bitcast_fusion.2, pred[]{:T(512)S(6)} %compare.4, pred[]{:T(512)S(6)} %lt.47), kind=kLoop, calls=%fused_computation.1.clone.1 | loop fusion | flops 524288 | bytes 1572902 | tf_op jit(solution)/shard_map/while/body/eval_jaxpr/jit(_where)/select_n | solution.py:23
  94.3 0.0 copy-done.1
  94.3 0.4 fusion.2
  94.7 0.4 multiply_reduce_fusion
  95.1 0.8 copy_bitcast_fusion.1
  (31 shorter events, 0.2 us)
Async XLA Ops:
  7.2 4.4 %copy-start = (bf16[64,1024]{1,0:T(8,128)(2,1)S(1)}, bf16[64,1024]{1,0:T(8,128)(2,1)}, u32[]{:S(2)}) copy-start(bf16[64,1024]{1,0:T(8,128)(2,1)} %param.12) | copy-start | bytes 393220
  7.2 77.4 %all-gather.4.cloned.1.call-start = ((), (), s32[]{:S(2)}) async-start(), calls=%async_computation.3 | async-start | bytes 4718592 | tf_op jit(solution)/shard_map/all_gather | solution.py:13
  26.5 4.4 %collective-permute-start = (bf16[64,128]{1,0:T(8,128)(2,1)S(1)}, bf16[64,128]{1,0:T(8,128)(2,1)S(1)}, u32[]{:S(2)}, u32[]{:S(2)}) collective-permute-start(bf16[64,128]{1,0:T(8,128)(2,1)S(1)} %bitcast.145), channel_id=1, source_target_pairs={{0,4},{4,8},{8,12},{12,16},{16,20},{20,24},{24,28},{28,0},{1,5},{5... | collective-permute-start | bytes 49160 | tf_op jit(solution)/shard_map/ppermute | solution.py:99
  30.8 4.6 %collective-permute-start.1 = (bf16[64,128]{1,0:T(8,128)(2,1)S(1)}, bf16[64,128]{1,0:T(8,128)(2,1)S(1)}, u32[]{:S(2)}, u32[]{:S(2)}) collective-permute-start(bf16[64,128]{1,0:T(8,128)(2,1)S(1)} %collective-permute-done), channel_id=1, source_target_pairs={{0,4},{4,8},{8,12},{12,16},{16,20},{20,24},{24,28},{28,0},{1,5},{5... | collective-permute-start | bytes 49160 | tf_op jit(solution)/shard_map/ppermute | solution.py:99
  32.2 35.1 %all-to-all-start.2 = ((bf16[16,4,128]{2,0,1:T(8,128)(2,1)}), bf16[16,4,128]{2,0,1:T(8,128)(2,1)S(1)}, u32[]{:S(2)}, u32[]{:S(2)}) async-start(bf16[16,4,128]{2,0,1:T(8,128)(2,1)} %copy_bitcast_fusion.3), calls=%async_computation.2 | async-start | bytes 32768 | tf_op jit(solution)/shard_map/all_to_all | solution.py:83
  35.4 4.1 %collective-permute-start.2 = (bf16[64,128]{1,0:T(8,128)(2,1)S(1)}, bf16[64,128]{1,0:T(8,128)(2,1)S(1)}, u32[]{:S(2)}, u32[]{:S(2)}) collective-permute-start(bf16[64,128]{1,0:T(8,128)(2,1)S(1)} %collective-permute-done.1), channel_id=1, source_target_pairs={{0,4},{4,8},{8,12},{12,16},{16,20},{20,24},{24,28},{28,0},{1,5},{5... | collective-permute-start | bytes 49160 | tf_op jit(solution)/shard_map/ppermute | solution.py:99
  39.6 4.3 %collective-permute-start.3 = (bf16[64,128]{1,0:T(8,128)(2,1)S(1)}, bf16[64,128]{1,0:T(8,128)(2,1)S(1)}, u32[]{:S(2)}, u32[]{:S(2)}) collective-permute-start(bf16[64,128]{1,0:T(8,128)(2,1)S(1)} %collective-permute-done.2), channel_id=1, source_target_pairs={{0,4},{4,8},{8,12},{12,16},{16,20},{20,24},{24,28},{28,0},{1,5},{5... | collective-permute-start | bytes 49160 | tf_op jit(solution)/shard_map/ppermute | solution.py:99
  43.9 4.4 %collective-permute-start.4 = (bf16[64,128]{1,0:T(8,128)(2,1)S(1)}, bf16[64,128]{1,0:T(8,128)(2,1)S(1)}, u32[]{:S(2)}, u32[]{:S(2)}) collective-permute-start(bf16[64,128]{1,0:T(8,128)(2,1)S(1)} %collective-permute-done.3), channel_id=1, source_target_pairs={{0,4},{4,8},{8,12},{12,16},{16,20},{20,24},{24,28},{28,0},{1,5},{5... | collective-permute-start | bytes 49160 | tf_op jit(solution)/shard_map/ppermute | solution.py:99
  48.3 19.0 %collective-permute-start.5 = (bf16[64,128]{1,0:T(8,128)(2,1)S(1)}, bf16[64,128]{1,0:T(8,128)(2,1)S(1)}, u32[]{:S(2)}, u32[]{:S(2)}) collective-permute-start(bf16[64,128]{1,0:T(8,128)(2,1)S(1)} %collective-permute-done.4), channel_id=1, source_target_pairs={{0,4},{4,8},{8,12},{12,16},{16,20},{20,24},{24,28},{28,0},{1,5},{5... | collective-permute-start | bytes 49160 | tf_op jit(solution)/shard_map/ppermute | solution.py:99
  67.3 14.4 %collective-permute-start.6 = (bf16[64,128]{1,0:T(8,128)(2,1)S(1)}, bf16[64,128]{1,0:T(8,128)(2,1)S(1)}, u32[]{:S(2)}, u32[]{:S(2)}) collective-permute-start(bf16[64,128]{1,0:T(8,128)(2,1)S(1)} %collective-permute-done.5), channel_id=1, source_target_pairs={{0,4},{4,8},{8,12},{12,16},{16,20},{20,24},{24,28},{28,0},{1,5},{5... | collective-permute-start | bytes 49160 | tf_op jit(solution)/shard_map/ppermute | solution.py:99
  67.3 14.6 %all-to-all-start.1 = ((bf16[16,4,1024]{2,0,1:T(8,128)(2,1)}), bf16[16,4,1024]{2,0,1:T(8,128)(2,1)S(1)}, u32[]{:S(2)}, u32[]{:S(2)}) async-start(bf16[16,4,1024]{2,0,1:T(8,128)(2,1)} %bitcast.137), calls=%async_computation.1 | async-start | bytes 262144 | tf_op jit(solution)/shard_map/all_to_all | solution.py:81
  83.3 11.0 %copy-start.1 = (bf16[64,1024]{1,0:T(8,128)(2,1)S(1)}, bf16[64,1024]{1,0:T(8,128)(2,1)}, u32[]{:S(2)}) copy-start(bf16[64,1024]{1,0:T(8,128)(2,1)} %param.10) | copy-start | bytes 393220
Sparse Core Ops, SparseCore 0:
  14.1 39.9 all-gather.3
